TPU v7x, 512 devices: a whole 4x8x8 slice. The times are simulated.
512 devices in a mesh: dp: 16 (over x, z_hi), code: 32 (over z_lo, y, core).
Axes of the slice: x: 4, y: 8, z: 8 (z_hi: 4, z_lo: 2; z = z_hi * 2 + z_lo), core: 2. Of those that a mesh axis runs over, the one named last changes fastest.
Arguments:
- tokens: bfloat16 [8192, 256], P('dp'), may hold values from -40 to 40
- codebook: bfloat16 [131072, 256], P('code'), may hold values from -6 to 6
- cotangent: bfloat16 [8192, 256], P('dp'), may hold values from -6 to 6
- index: int32 [8192], P('dp'), may hold values from 0 to 131071
Outputs:
- quantized: bfloat16 [8192, 256], P('dp')
- token_grad: bfloat16 [8192, 256], P('dp')
- codebook_grad: bfloat16 [131072, 256], P(('code', 'dp'))
- code_usage: float32 [131072], P(('code', 'dp'))
- entropy_loss: float32 [], replicated
All inputs are finite; a program needn't handle non-finite values.
Results may differ from a plain program's by a relative error of at most 0.012.
Values may be sent and summed in bfloat16 or wider, within the bound.
A program may use at most 64 MiB of HBM per device.

v0:
```python
import jax
import jax.numpy as jnp
from jax import lax
from jax.sharding import PartitionSpec as P


def body(tokens, codebook, cotangent, index):
    token_rows, features = tokens.shape
    code_rows = codebook.shape[0]
    scale_factor = float(features) ** (-0.5)
    code_devices = lax.axis_size("code")
    data_devices = lax.axis_size("dp")
    offset = lax.axis_index("code") * code_rows
    block_length = min(1024, code_rows)
    block_count = code_rows // block_length
    stacked = codebook.reshape(block_count, block_length, features)
    local_ids = index - offset
    inside = (local_ids >= 0) & (local_ids < code_rows)
    picked = jnp.take(codebook, jnp.where(inside, local_ids, 0), axis=0)
    picked = jnp.where(inside[:, None], picked.astype(jnp.float32), 0.0)
    quantized = lax.psum(picked.astype(jnp.bfloat16), "code")
    chosen_sums = jax.ops.segment_sum(
        cotangent.astype(jnp.float32),
        jnp.where(inside, local_ids, code_rows),
        num_segments=code_rows + 1,
    )[:code_rows]

    def scores(code_block):
        logits = (
            jnp.einsum("td,kd->tk", tokens, code_block, preferred_element_type=jnp.float32)
            * scale_factor
        )
        sensed = jnp.einsum("td,kd->tk", cotangent, code_block, preferred_element_type=jnp.float32)
        return (logits, sensed)

    def block_totals(code_block):
        logits, sensed = scores(code_block)
        row_top = jnp.max(logits, axis=1)
        weights = jnp.exp(logits - row_top[:, None])
        return (
            row_top,
            jnp.sum(weights, axis=1),
            jnp.sum(weights * sensed, axis=1),
            jnp.sum(weights * logits, axis=1),
        )

    block_tops, block_sums, sensed_sums, logit_sums = lax.map(block_totals, stacked)
    local_peak = jnp.max(block_tops, axis=0)
    factor = jnp.exp(block_tops - local_peak[None, :])
    local_stats = (
        local_peak,
        jnp.sum(block_sums * factor, axis=0),
        jnp.sum(sensed_sums * factor, axis=0),
        jnp.sum(logit_sums * factor, axis=0),
    )
    row_peak = lax.pmax(local_stats[0], "code")
    rescale = jnp.exp(local_stats[0] - row_peak)
    row_total, sensed_total, logit_total = lax.psum(
        (local_stats[1] * rescale, local_stats[2] * rescale, local_stats[3] * rescale), "code"
    )
    row_dot = sensed_total / row_total
    token_entropy = jnp.log(row_total) + row_peak - logit_total / row_total

    def block_grads(code_block):
        logits, sensed = scores(code_block)
        probs = jnp.exp(logits - row_peak[:, None]) / row_total[:, None]
        logit_grad = (probs * (sensed - row_dot[:, None])).astype(jnp.bfloat16)
        return (probs, logit_grad)

    def gradient_step(running, code_block):
        probs, logit_grad = block_grads(code_block)
        running = running + jnp.dot(logit_grad, code_block, preferred_element_type=jnp.float32)
        usage_part = jnp.sum(probs, axis=0)
        grad_term = scale_factor * jnp.einsum(
            "tk,td->kd", logit_grad, tokens, preferred_element_type=jnp.float32
        )
        return (running, (usage_part, grad_term))

    running, outputs = lax.scan(
        gradient_step, jnp.zeros((token_rows, features), jnp.float32), stacked
    )
    usage_local = outputs[0].reshape(code_rows)
    code_local = outputs[1].reshape(code_rows, features) + chosen_sums
    code_sum = lax.psum_scatter(
        code_local.astype(jnp.bfloat16), "dp", scatter_dimension=0, tiled=True
    )
    usage_sum = lax.psum_scatter(usage_local, "dp", scatter_dimension=0, tiled=True)
    token_grad = (lax.psum(running, "code") * scale_factor).astype(jnp.bfloat16)
    tokens_total = token_rows * data_devices
    codes_total = code_rows * code_devices
    code_usage = usage_sum * (codes_total / tokens_total)
    shares = usage_sum / tokens_total
    local_loss = jnp.sum(token_entropy) / (tokens_total * code_devices) + jnp.sum(
        jax.scipy.special.xlogy(shares, shares)
    )
    entropy_loss = lax.psum(local_loss, ("dp", "code"))
    return (quantized, token_grad, code_sum, code_usage, entropy_loss)


def solution(mesh):
    placed = (P("dp", None), P("code", None), P("dp", None), P("dp"))
    return jax.shard_map(
        body,
        mesh=mesh,
        in_specs=placed,
        out_specs=(P("dp", None), P("dp", None), P(("code", "dp"), None), P(("code", "dp")), P()),
        check_vma=False,
    )
```

profile of v0, /device:TPU:1, one launch (start us, length us, event | category | flops | bytes accessed | tf_op | source)
XLA Modules:
  0.0 632.0 jit_solution(5439487695934471928)
XLA Ops:
  8.1 16.1 %while.31 = (s32[]{:T(128)}, f32[4,512]{1,0:T(4,128)S(1)}, f32[4,512]{1,0:T(4,128)S(1)}, f32[4,512]{1,0:T(4,128)S(1)}, f32[4,512]{1,0:T(4,128)S(1)}, /*index=5*/...) while((s32[]{:T(128)}, f32[4,512]{1,0:T(4,128)S(1)}, ...), condition=%wide.region_6.7_spmd, body=%wide.region_1.0_spmd.sunk | while | flops 542636032 | bytes 8941729 | solution.py:47
  8.1 1.6 multiply_reduce_fusion.5
  12.2 1.6 multiply_reduce_fusion.5
  16.2 1.6 multiply_reduce_fusion.5
  20.2 1.6 multiply_reduce_fusion.5
  24.2 59.2 %pmax.7 = f32[512]{0:T(512)S(1)} all-reduce(f32[512]{0:T(512)S(1)} %reduce_max.18), channel_id=1, replica_groups=mesh['dp'=16,'code'=32] {'code'}, use_global_device_ids=true, to_apply=%region_8.9 | all-reduce | flops 512 | bytes 4096 | tf_op jit(solution)/shard_map/pmax | solution.py:56
  83.5 53.9 %all-reduce.1 = (f32[512]{0:T(512)S(1)}, f32[512]{0:T(512)S(1)}, f32[512]{0:T(512)S(1)}) all-reduce(f32[512]{0:T(512)S(1)} %get-tuple-element.198, f32[512]{0:T(512)S(1)} %get-tuple-element.197, f32[512]{0:T(512)S(1)} %get-tuple-element.196), channel_id=1, replica_groups=mesh['dp'=16,'code'=32] {'code'}, use_global_device_ids=true, to_apply=%region_10.11 | all-reduce | flops 1536 | bytes 12288 | tf_op jit(solution)/shard_map/psum | solution.py:58
  138.0 24.0 %while.32 = (s32[]{:T(128)}, f32[512,256]{1,0:T(8,128)}, f32[4,1024]{1,0:T(4,128)S(1)}, f32[4,1024,256]{2,1,0:T(8,128)}, bf16[4,1024,256]{2,1,0:T(8,128)(2,1)}, ...) while((s32[]{:T(128)}, f32[512,256]{1,0:T(8,128)}, ...), condition=%wide.region_15.16_spmd.clone, body=%wide.region_13.15_spmd.clone.sunk | while | flops 1077935104 | bytes 22300912 | solution.py:79
  138.0 1.9 fusion.64
  143.3 1.9 fusion.64
  145.8 2.3 convolution_add_fusion.2
  149.5 1.9 fusion.64
  152.0 2.3 convolution_add_fusion.2
  155.8 1.9 fusion.64
  158.3 2.3 convolution_add_fusion.2
  162.2 3.4 gather_fusion
  166.6 6.4 %scatter_custom_fusion = f32[4097,256]{1,0:T(8,128)} fusion(s32[512]{0:T(512)S(1)} %subtract_select_fusion, f32[]{:T(128)} %constant.46.clone.1, bf16[512,256]{1,0:T(8,128)(2,1)S(1)} %copy-done.3), kind=kCustom, calls=%fused_computation.34 | custom fusion | flops 262144 | bytes 4457476 | tf_op jit(solution)/shard_map/scatter-add | solution.py:22
  173.0 5.3 fusion.22
  180.9 73.2 %all-reduce = f32[4096]{0:T(1024)S(1)} all-reduce(f32[4096]{0:T(1024)S(1)} %bitcast.105), channel_id=3, replica_groups=mesh['dp'=16,'code'=32] {'dp'}, use_global_device_ids=true, to_apply=%region_19.20.clone | all-reduce | flops 4096 | bytes 32768
  256.0 106.5 %psum.47 = f32[]{:T(128)} all-reduce(f32[]{:T(128)S(6)} %add.45), channel_id=1, replica_groups=mesh['dp'=16,'code'=32] {'dp','code'}, use_global_device_ids=true, to_apply=%region_24.25 | all-reduce | flops 1 | bytes 8 | tf_op jit(solution)/shard_map/psum | solution.py:96
  362.5 29.0 %all-reduce.7.cloned.1.call-done = f32[512,256]{1,0:T(8,128)} async-done(((f32[512,256]{1,0:T(8,128)}), f32[512,256]{1,0:T(8,128)}) %all-reduce.7.cloned.1.call-update) | async-done | bytes 524304 | tf_op jit(solution)/shard_map/psum | solution.py:88
  391.4 1.8 multiply_convert_fusion.1
  393.2 229.7 %all-reduce.5.cloned.1.call-done = bf16[512,256]{1,0:T(8,128)(2,1)} async-done(((bf16[512,256]{1,0:T(8,128)(2,1)}), bf16[512,256]{1,0:T(8,128)(2,1)}) %all-reduce.5.cloned.1.call-update) | async-done | bytes 262160 | tf_op jit(solution)/shard_map/psum | solution.py:21
  622.9 1.7 copy.51
  (98 shorter events, 23.0 us)
Async XLA Ops:
  8.0 383.4 %all-reduce.7.cloned.1.call-start = ((), (), s32[]{:S(2)}) async-start(), calls=%async_computation.2 | async-start | bytes 1048576 | tf_op jit(solution)/shard_map/psum | solution.py:88
  8.1 1.6 copy-start.1
  12.1 1.6 copy-start.1
  16.2 1.6 copy-start.1
  20.2 1.7 copy-start.1
  138.0 24.1 %copy-start.5 = (s32[512]{0:T(512)S(1)}, s32[512]{0:T(512)}, u32[]{:S(2)}) copy-start(s32[512]{0:T(512)} %param.11) | copy-start | bytes 6148
  138.0 1.9 copy-start
  138.0 1.9 copy-start.2
  140.5 1.3 copy-start.4
  143.3 1.9 copy-start
  143.3 1.9 copy-start.2
  145.7 2.4 copy-start.4
  149.5 1.9 copy-start
  149.5 1.9 copy-start.2
  151.9 2.4 copy-start.4
  155.8 1.9 copy-start
  155.8 1.9 copy-start.2
  158.2 2.4 copy-start.4
  162.0 4.6 copy-start.3
  162.1 460.8 %all-reduce.5.cloned.1.call-start = ((), (), s32[]{:S(2)}) async-start(), calls=%async_computation.1 | async-start | bytes 524288 | tf_op jit(solution)/shard_map/psum | solution.py:21
  166.5 456.4 %reduce-scatter.2.cloned.1.call-start = ((), (), s32[]{:S(2)}) async-start(), calls=%async_computation.3 | async-start | bytes 2228224 | tf_op jit(solution)/shard_map/reduce_scatter | solution.py:84
Sparse Core Ops, SparseCore 0:
  162.2 229.1 all-reduce.6
  394.9 227.9 all-reduce.4
Sparse Core Ops, SparseCore 1:
  178.4 91.8 reduce-scatter.1
where the time goes:
time: 633 us; the launch traced here: 632 us
  blocking collectives  293 us (46%)
  waiting for transfers between devices  259 us (41%)
  matrix products  36.4 us (6%)
  other arithmetic  18.4 us (3%)
  between operations  17.6 us (3%)
  local copies, waits for them, and re-layouts  7.52 us (1%)
    psum x1, waiting for transfers between devices, body(): quantized = lax.psum(picked.astype(jnp.bfloat16), 'code')  230 us
    psum x1, blocking collectives, body(): entropy_loss = lax.psum(local_loss, ('dp', 'code'))  106 us
    unnamed x1, blocking collectives  73.2 us
    pmax x1, blocking collectives, body(): row_peak = lax.pmax(local_stats[0], 'code')  59.2 us
    psum x1, blocking collectives, body(): lax.psum((local_stats[1] * rescale, local_stats[2] * rescale, local_stats...  53.9 us
    psum x1, waiting for transfers between devices, body(): token_grad = (lax.psum(running, 'code') * scale_factor).astype(jnp.bfloat16)  29 us
    dot_general x8, matrix products, scores(): jnp.einsum('td,kd->tk', tokens, code_block, preferred_element_type=jnp.fl...  14.2 us
  transfers between devices with their start and end apart: 3, of which 2 were waited for; matrix products, arithmetic and copies ran while one was open for 3% of the time, Pallas kernels for 0%

commit v1 on v0

v1 whole, which is shorter than its diff:
```python
import functools

import jax
import jax.numpy as jnp
from jax import lax
from jax.experimental import pallas as pl
from jax.experimental.pallas import tpu as pltpu
from jax.sharding import PartitionSpec as P

MESH = pl.DeviceIdType.MESH
F32 = jnp.float32
BF16 = jnp.bfloat16
RING = 4
VMEM_BYTES = 60 * 1024 * 1024


def dot(a, b, dims):
    return lax.dot_general(a, b, (dims, ((), ())), preferred_element_type=F32)


def vmem():
    return pl.BlockSpec(memory_space=pltpu.VMEM)


def totals_kernel(scale, code_rows, tok_ref, cot_ref, idx_ref, cb_ref, st_ref, q_ref, run, qacc):
    step = pl.program_id(0)
    steps = pl.num_programs(0)
    block = cb_ref.shape[0]

    @pl.when(step == 0)
    def _():
        run[0:1, :] = jnp.full_like(run[0:1, :], -jnp.inf)
        run[1:4, :] = jnp.zeros_like(run[1:4, :])
        qacc[...] = jnp.zeros_like(qacc)

    codes = cb_ref[...]
    logits = dot(codes, tok_ref[...], ((1,), (1,)))
    sensed = dot(codes, cot_ref[...], ((1,), (1,)))
    old = run[0:1, :]
    top = jnp.maximum(old, jnp.max(logits, axis=0, keepdims=True))
    weights = jnp.exp((logits - top) * scale)
    factor = jnp.exp((old - top) * scale)
    run[0:1, :] = top
    run[1:2, :] = run[1:2, :] * factor + jnp.sum(weights, axis=0, keepdims=True)
    run[2:3, :] = run[2:3, :] * factor + jnp.sum(weights * sensed, axis=0, keepdims=True)
    run[3:4, :] = run[3:4, :] * factor + jnp.sum(weights * logits, axis=0, keepdims=True)
    first = lax.axis_index("code") * code_rows + step * block
    rows = lax.broadcasted_iota(jnp.int32, logits.shape, 0)
    hot = jnp.where(rows == idx_ref[...] - first, 1.0, 0.0).astype(BF16)
    qacc[...] += dot(codes, hot, ((0,), (0,)))

    @pl.when(step == steps - 1)
    def _():
        st_ref[...] = run[...]
        q_ref[...] = qacc[...].T.astype(BF16)


def totals(tokens, cotangent, index, codebook, scale, block):
    rows, width = tokens.shape
    code_rows = codebook.shape[0]
    whole = lambda i: (0, 0)
    return pl.pallas_call(
        functools.partial(totals_kernel, scale, code_rows),
        grid=(code_rows // block,),
        out_shape=(
            jax.ShapeDtypeStruct((4, rows), F32),
            jax.ShapeDtypeStruct((rows, width), BF16),
        ),
        in_specs=[
            pl.BlockSpec((rows, width), whole),
            pl.BlockSpec((rows, width), whole),
            pl.BlockSpec((1, rows), whole),
            pl.BlockSpec((block, width), lambda i: (i, 0)),
        ],
        out_specs=(pl.BlockSpec((4, rows), whole), pl.BlockSpec((rows, width), whole)),
        scratch_shapes=[pltpu.VMEM((4, rows), F32), pltpu.VMEM((width, rows), F32)],
        compiler_params=pltpu.CompilerParams(vmem_limit_bytes=VMEM_BYTES),
        name="totals",
    )(tokens, cotangent, index, codebook)


def stats_kernel(scale, chips, st_ref, out_ref, pair_buf, mine, chip_buf, psend, precv, send, recv):
    dp = lax.axis_index("dp")
    code = lax.axis_index("code")
    core, chip = code % 2, code // 2
    partner = (dp, chip * 2 + 1 - core)
    peers = [(dp, ((chip + j) % chips) * 2 + core) for j in range(1, chips)]
    barrier = pltpu.get_barrier_semaphore()
    for peer in [partner] + peers:
        pl.semaphore_signal(barrier, inc=1, device_id=peer, device_id_type=MESH)
    pl.semaphore_wait(barrier, chips)

    swap = pltpu.make_async_remote_copy(
        src_ref=st_ref, dst_ref=pair_buf, send_sem=psend, recv_sem=precv,
        device_id=partner, device_id_type=MESH,
    )
    swap.start()
    swap.wait()
    one, two = st_ref[...], pair_buf[...]
    top = jnp.maximum(one[0:1], two[0:1])
    sums = one[1:4] * jnp.exp((one[0:1] - top) * scale) + two[1:4] * jnp.exp((two[0:1] - top) * scale)
    mine[0:1, :] = top
    mine[1:4, :] = sums
    copies = []
    for j, peer in enumerate(peers):
        copy = pltpu.make_async_remote_copy(
            src_ref=mine, dst_ref=chip_buf.at[chip], send_sem=send.at[j], recv_sem=recv.at[j],
            device_id=peer, device_id_type=MESH,
        )
        copy.start()
        copies.append(copy)
    chip_buf[pl.ds(chip, 1), :, :] = mine[...][None]
    for copy in copies:
        copy.wait()
    tops = [chip_buf[j, 0:1, :] for j in range(chips)]
    peak = functools.reduce(jnp.maximum, tops)
    total = sum(chip_buf[j, 1:4, :] * jnp.exp((tops[j] - peak) * scale) for j in range(chips))
    weight = total[0:1]
    inverse = 1.0 / weight
    out_ref[0:1, :] = peak
    out_ref[1:2, :] = inverse
    out_ref[2:3, :] = total[1:2] / weight
    out_ref[3:4, :] = jnp.log(weight) + (peak - total[2:3] / weight) * scale


def row_stats(local, scale, chips):
    shape = local.shape
    return pl.pallas_call(
        functools.partial(stats_kernel, scale, chips),
        out_shape=jax.ShapeDtypeStruct(shape, F32),
        in_specs=[vmem()],
        out_specs=vmem(),
        scratch_shapes=[
            pltpu.VMEM(shape, F32),
            pltpu.VMEM(shape, F32),
            pltpu.VMEM((chips,) + shape, F32),
            pltpu.SemaphoreType.DMA,
            pltpu.SemaphoreType.DMA,
            pltpu.SemaphoreType.DMA((chips - 1,)),
            pltpu.SemaphoreType.DMA((chips - 1,)),
        ],
        compiler_params=pltpu.CompilerParams(collective_id=0, has_side_effects=True),
        name="row_stats",
    )(local)


def grads_kernel(scale, code_rows, tok_ref, cot_ref, idx_ref, st_ref, cb_ref, cg_ref, us_ref, tg_ref, acc):
    step = pl.program_id(0)
    steps = pl.num_programs(0)
    block = cb_ref.shape[0]

    @pl.when(step == 0)
    def _():
        acc[...] = jnp.zeros_like(acc)

    codes = cb_ref[...]
    tok = tok_ref[...]
    cot = cot_ref[...]
    logits = dot(codes, tok, ((1,), (1,)))
    sensed = dot(codes, cot, ((1,), (1,)))
    probs = jnp.exp((logits - st_ref[0:1, :]) * scale) * st_ref[1:2, :]
    grad = (probs * (sensed - st_ref[2:3, :])).astype(BF16)
    acc[...] += dot(codes, grad, ((0,), (0,)))
    first = lax.axis_index("code") * code_rows + step * block
    rows = lax.broadcasted_iota(jnp.int32, logits.shape, 0)
    hot = jnp.where(rows == idx_ref[...] - first, 1.0, 0.0).astype(BF16)
    cg_ref[...] = (dot(grad, tok, ((1,), (0,))) * scale + dot(hot, cot, ((1,), (0,)))).astype(BF16)
    lanes = min(128, probs.shape[1])
    part = sum(probs[:, i : i + lanes] for i in range(0, probs.shape[1], lanes))
    usage = jnp.sum(part.T, axis=0, keepdims=True)
    span = us_ref.shape[2]
    for i in range(us_ref.shape[0]):
        us_ref[i, :, :] = usage[:, i * span : (i + 1) * span]

    @pl.when(step == steps - 1)
    def _():
        tg_ref[...] = (acc[...] * scale).T.astype(BF16)


def grads(tokens, cotangent, index, stats, codebook, scale, block, data_devices):
    rows, width = tokens.shape
    code_rows = codebook.shape[0]
    span = code_rows // data_devices
    whole = lambda i: (0, 0)
    return pl.pallas_call(
        functools.partial(grads_kernel, scale, code_rows),
        grid=(code_rows // block,),
        out_shape=(
            jax.ShapeDtypeStruct((code_rows, width), BF16),
            jax.ShapeDtypeStruct((data_devices, 1, span), F32),
            jax.ShapeDtypeStruct((rows, width), BF16),
        ),
        in_specs=[
            pl.BlockSpec((rows, width), whole),
            pl.BlockSpec((rows, width), whole),
            pl.BlockSpec((1, rows), whole),
            pl.BlockSpec((4, rows), whole),
            pl.BlockSpec((block, width), lambda i: (i, 0)),
        ],
        out_specs=(
            pl.BlockSpec((block, width), lambda i: (i, 0)),
            pl.BlockSpec((block // span, 1, span), lambda i: (i, 0, 0)),
            pl.BlockSpec((rows, width), whole),
        ),
        scratch_shapes=[pltpu.VMEM((width, rows), F32)],
        compiler_params=pltpu.CompilerParams(vmem_limit_bytes=VMEM_BYTES),
        name="grads",
    )(tokens, cotangent, index, stats, codebook)


def sums_kernel(
    chips, tokens_total, codes_total,
    q_ref, tg_ref, cg_ref, us_ref, st_ref,
    qo_ref, tgo_ref, cgo_ref, uso_ref, loss_ref,
    t_in, t_half, t_piece, t_sum, t_full,
    x_hop, x_out, x_got, z_part, z_hop, z_out, z_got,
    u_buf, l_own, l_dp, l_core, l_pair, l_chip,
    t_send, t_recv, p_send, p_recv, g_send, g_recv, f_send, f_recv,
    x_send, x_recv, z_send, z_recv,
    u_send, u_recv, ld_send, ld_recv, lc_send, lc_recv, lg_send, lg_recv,
):
    dp = lax.axis_index("dp")
    code = lax.axis_index("code")
    core, chip = code % 2, code // 2
    xi, zi = dp // RING, dp % RING
    data = RING * RING
    rows = q_ref.shape[0]
    half = rows // 2
    piece = half // chips
    span = cg_ref.shape[0] // data
    hs = span // 2

    partner = (dp, chip * 2 + 1 - core)
    peers = [(dp, ((chip + j) % chips) * 2 + core) for j in range(1, chips)]
    mates = [((dp + j) % data, code) for j in range(1, data)]
    xn = {d: (((xi + d) % RING) * RING + zi, code) for d in (1, 3)}
    zn = {d: (xi * RING + (zi + d) % RING, code) for d in (1, 3)}

    barrier = pltpu.get_barrier_semaphore()
    for peer in [partner] + peers + mates:
        pl.semaphore_signal(barrier, inc=1, device_id=peer, device_id_type=MESH)
    pl.semaphore_wait(barrier, chips + data - 1)

    def send(src, dst, ssem, rsem, peer):
        copy = pltpu.make_async_remote_copy(
            src_ref=src, dst_ref=dst, send_sem=ssem, recv_sem=rsem, device_id=peer, device_id_type=MESH
        )
        copy.start()
        return copy

    u_copies = [
        send(us_ref.at[(dp + j) % data], u_buf.at[dp], u_send.at[j - 1], u_recv.at[j - 1], mates[j - 1])
        for j in range(1, data)
    ]
    theirs = pl.ds(pl.multiple_of((1 - core) * half, half), half)
    ours = pl.ds(pl.multiple_of(core * half, half), half)
    t_copies = [
        send(ref.at[theirs], t_in.at[i], t_send.at[i], t_recv.at[i], partner)
        for i, ref in enumerate((tg_ref, q_ref))
    ]

    order = [(zi + d) % RING for d in (2, 1, 3, 0)]
    x_copies = {}
    z_copies = {}

    def part(xd, k, side):
        start = (((xi + xd) % RING) * RING + order[k]) * span + side * hs
        return pl.ds(pl.multiple_of(start, hs), hs)

    def x_first(k):
        x_copies[k, 0] = send(cg_ref.at[part(2, k, 0)], x_hop.at[k, 0], x_send.at[k, 0], x_recv.at[k, 0], xn[1])
        x_copies[k, 1] = send(cg_ref.at[part(2, k, 1)], x_hop.at[k, 1], x_send.at[k, 1], x_recv.at[k, 1], xn[3])

    def x_direct(k):
        x_copies[k, 2] = send(cg_ref.at[part(1, k, 1)], x_got.at[k, 1], x_send.at[k, 2], x_recv.at[k, 2], xn[1])
        x_copies[k, 3] = send(cg_ref.at[part(3, k, 0)], x_got.at[k, 0], x_send.at[k, 3], x_recv.at[k, 3], xn[3])

    def x_second(k):
        x_copies[k, 0].wait_recv()
        x_out[k, 0] = (x_hop[k, 0].astype(F32) + cg_ref[part(1, k, 0), :].astype(F32)).astype(BF16)
        x_copies[k, 4] = send(x_out.at[k, 0], x_got.at[k, 3], x_send.at[k, 4], x_recv.at[k, 4], xn[1])
        x_copies[k, 1].wait_recv()
        x_out[k, 1] = (x_hop[k, 1].astype(F32) + cg_ref[part(3, k, 1), :].astype(F32)).astype(BF16)
        x_copies[k, 5] = send(x_out.at[k, 1], x_got.at[k, 2], x_send.at[k, 5], x_recv.at[k, 5], xn[3])

    def x_third(k):
        for i in (2, 3, 4, 5):
            x_copies[k, i].wait_recv()
        low = cg_ref[part(0, k, 0), :].astype(F32) + x_got[k, 0].astype(F32) + x_got[k, 3].astype(F32)
        high = cg_ref[part(0, k, 1), :].astype(F32) + x_got[k, 1].astype(F32) + x_got[k, 2].astype(F32)
        return low, high

    def z_store(k):
        low, high = x_third(k)
        z_part[k, 0] = low.astype(BF16)
        z_part[k, 1] = high.astype(BF16)

    def z_first():
        z_store(0)
        z_copies[0] = send(z_part.at[0, 0], z_hop.at[0], z_send.at[0], z_recv.at[0], zn[1])
        z_copies[1] = send(z_part.at[0, 1], z_hop.at[1], z_send.at[1], z_recv.at[1], zn[3])

    def z_second_up():
        z_store(1)
        z_copies[2] = send(z_part.at[1, 1], z_got.at[1], z_send.at[2], z_recv.at[2], zn[1])
        z_copies[0].wait_recv()
        z_out[0] = (z_hop[0].astype(F32) + z_part[1, 0].astype(F32)).astype(BF16)
        z_copies[4] = send(z_out.at[0], z_got.at[3], z_send.at[4], z_recv.at[4], zn[1])

    def z_second_down():
        z_store(2)
        z_copies[3] = send(z_part.at[2, 0], z_got.at[0], z_send.at[3], z_recv.at[3], zn[3])
        z_copies[1].wait_recv()
        z_out[1] = (z_hop[1].astype(F32) + z_part[2, 1].astype(F32)).astype(BF16)
        z_copies[5] = send(z_out.at[1], z_got.at[2], z_send.at[5], z_recv.at[5], zn[3])

    def z_third():
        low, high = x_third(3)
        for i in (2, 3, 4, 5):
            z_copies[i].wait_recv()
        cgo_ref[0:hs, :] = (low + z_got[0].astype(F32) + z_got[3].astype(F32)).astype(BF16)
        cgo_ref[hs:, :] = (high + z_got[1].astype(F32) + z_got[2].astype(F32)).astype(BF16)

    x_first(0)
    x_direct(0)
    x_first(1)

    for i, ref in enumerate((tg_ref, q_ref)):
        t_copies[i].wait_recv()
        t_half[i] = (t_in[i].astype(F32) + ref[ours, :].astype(F32)).astype(BF16)

    def rows_of(j):
        return pl.ds(pl.multiple_of(((chip + j) % chips) * piece, piece), piece)

    p_copies = [
        send(t_half.at[:, rows_of(j)], t_piece.at[j], p_send.at[j - 1], p_recv.at[j - 1], peers[j - 1])
        for j in range(1, chips)
    ]

    x_second(0)
    x_direct(1)
    x_first(2)

    u_buf[pl.ds(dp, 1), :, :] = us_ref[pl.ds(dp, 1), :, :]
    for copy in u_copies:
        copy.wait_recv()
    usage = sum(u_buf[j] for j in range(data))
    uso_ref[...] = usage * (codes_total / tokens_total)
    shares = usage / tokens_total
    terms = jnp.where(shares > 0, shares * jnp.log(jnp.where(shares > 0, shares, 1.0)), 0.0)
    local = jnp.sum(st_ref[3:4, :]) / (tokens_total * chips * 2) + jnp.sum(terms)
    l_own[...] = jnp.full(l_own.shape, local, F32)
    l_dp[pl.ds(dp, 1), :, :] = l_own[...][None]
    ld_copies = [
        send(l_own, l_dp.at[dp], ld_send.at[j - 1], ld_recv.at[j - 1], mates[j - 1]) for j in range(1, data)
    ]

    x_second(1)
    x_direct(2)
    x_first(3)

    for copy in p_copies:
        copy.wait_recv()
    mine = rows_of(0)
    total = t_half[:, mine, :].astype(F32)
    for j in range(1, chips):
        total = total + t_piece[j].astype(F32)
    t_sum[...] = total.astype(BF16)
    base = core * half
    spot = pl.ds(pl.multiple_of(base + chip * piece, piece), piece)
    g_copies = [
        send(t_sum, t_full.at[:, spot], g_send.at[j - 1], g_recv.at[j - 1], peers[j - 1]) for j in range(1, chips)
    ]
    t_full[:, spot, :] = t_sum[...]

    z_first()
    x_second(2)
    x_direct(3)

    for copy in ld_copies:
        copy.wait_recv()
    l_core[...] = sum(l_dp[j] for j in range(data))
    lc_copy = send(l_core, l_pair, lc_send, lc_recv, partner)

    z_second_up()
    x_second(3)

    for copy in g_copies:
        copy.wait_recv()
    f_copy = send(t_full.at[:, ours], t_full.at[:, ours], f_send, f_recv, partner)

    lc_copy.wait_recv()
    l_chip[pl.ds(chip, 1), :, :] = (l_core[...] + l_pair[...])[None]
    lg_copies = [
        send(l_chip.at[chip], l_chip.at[chip], lg_send.at[j - 1], lg_recv.at[j - 1], peers[j - 1])
        for j in range(1, chips)
    ]

    z_second_down()
    z_third()

    f_copy.wait_recv()
    tgo_ref[...] = t_full[0]
    qo_ref[...] = t_full[1]
    for copy in lg_copies:
        copy.wait_recv()
    loss_ref[...] = sum(l_chip[j] for j in range(chips))

    pending = u_copies + t_copies + p_copies + ld_copies + g_copies + lg_copies + [lc_copy, f_copy]
    for copy in pending + list(x_copies.values()) + list(z_copies.values()):
        copy.wait_send()


def final_sums(q_part, tg_part, cg_part, usage_part, stats, chips, tokens_total, codes_total):
    rows, width = q_part.shape
    data = RING * RING
    span = cg_part.shape[0] // data
    hs = span // 2
    half = rows // 2
    piece = half // chips
    dma = pltpu.SemaphoreType.DMA
    return pl.pallas_call(
        functools.partial(sums_kernel, chips, tokens_total, codes_total),
        out_shape=(
            jax.ShapeDtypeStruct((rows, width), BF16),
            jax.ShapeDtypeStruct((rows, width), BF16),
            jax.ShapeDtypeStruct((span, width), BF16),
            jax.ShapeDtypeStruct((1, span), F32),
            jax.ShapeDtypeStruct((1, 128), F32),
        ),
        in_specs=[vmem()] * 5,
        out_specs=(vmem(),) * 5,
        scratch_shapes=[
            pltpu.VMEM((2, half, width), BF16),
            pltpu.VMEM((2, half, width), BF16),
            pltpu.VMEM((chips, 2, piece, width), BF16),
            pltpu.VMEM((2, piece, width), BF16),
            pltpu.VMEM((2, rows, width), BF16),
            pltpu.VMEM((RING, 2, hs, width), BF16),
            pltpu.VMEM((RING, 2, hs, width), BF16),
            pltpu.VMEM((RING, 4, hs, width), BF16),
            pltpu.VMEM((RING - 1, 2, hs, width), BF16),
            pltpu.VMEM((2, hs, width), BF16),
            pltpu.VMEM((2, hs, width), BF16),
            pltpu.VMEM((4, hs, width), BF16),
            pltpu.VMEM((data, 1, span), F32),
            pltpu.VMEM((1, 128), F32),
            pltpu.VMEM((data, 1, 128), F32),
            pltpu.VMEM((1, 128), F32),
            pltpu.VMEM((1, 128), F32),
            pltpu.VMEM((chips, 1, 128), F32),
            dma((2,)), dma((2,)),
            dma((chips - 1,)), dma((chips - 1,)),
            dma((chips - 1,)), dma((chips - 1,)),
            dma, dma,
            dma((RING, 6)), dma((RING, 6)),
            dma((6,)), dma((6,)),
            dma((data - 1,)), dma((data - 1,)),
            dma((data - 1,)), dma((data - 1,)),
            dma, dma,
            dma((chips - 1,)), dma((chips - 1,)),
        ],
        compiler_params=pltpu.CompilerParams(
            collective_id=1, has_side_effects=True, vmem_limit_bytes=VMEM_BYTES
        ),
        name="final_sums",
    )(q_part, tg_part, cg_part, usage_part, stats)


def body(block, tokens, codebook, cotangent, index):
    token_rows, features = tokens.shape
    code_rows = codebook.shape[0]
    scale = float(features) ** (-0.5)
    code_devices = lax.axis_size("code")
    data_devices = lax.axis_size("dp")
    chips = code_devices // 2
    index = index.reshape(1, token_rows)
    local, q_part = totals(tokens, cotangent, index, codebook, scale, block)
    stats = row_stats(local, scale, chips)
    cg_part, usage_part, tg_part = grads(
        tokens, cotangent, index, stats, codebook, scale, block, data_devices
    )
    quantized, token_grad, code_sum, code_usage, loss = final_sums(
        q_part, tg_part, cg_part, usage_part, stats, chips,
        token_rows * data_devices, code_rows * code_devices,
    )
    return (quantized, token_grad, code_sum, code_usage.reshape(-1), loss[0, 0])


def solution(mesh, block=512):
    placed = (P("dp", None), P("code", None), P("dp", None), P("dp"))
    return jax.shard_map(
        functools.partial(body, block),
        mesh=mesh,
        in_specs=placed,
        out_specs=(P("dp", None), P("dp", None), P(("code", "dp"), None), P(("code", "dp")), P()),
        check_vma=False,
    )
```

time: 633 us -> 91.9 us (0.15)
  blocking collectives: 293 us -> 0 us
  waiting for transfers between devices: 259 us -> 0 us
  Pallas kernels: 0 us -> 82.9 us
  matrix products: 36.4 us -> 0 us
  other arithmetic: 18.4 us -> 0 us
  between operations: 17.6 us -> 2.35 us
    psum x2 -> x0, waiting for transfers between devices: 259 us -> none  [the longest x1 230 us: body(): quantized = lax.psum(picked.astype(jnp.bfloat16), 'code')]
    psum x2 -> x0, blocking collectives: 160 us -> none  [the longest x1 106 us: body(): entropy_loss = lax.psum(local_loss, ('dp', 'code'))]
    pallas_call x0 -> x4, Pallas kernels: none -> 82.9 us  [the longest x1 43 us: final_sums(): pl.pallas_call(functools.partial(sums_kernel, chips, tokens_total, codes_...]
    unnamed x1 -> x0, blocking collectives: 73.2 us -> none
    pmax x1 -> x0, blocking collectives: 59.2 us -> none  [body(): row_peak = lax.pmax(local_stats[0], 'code')]
    dot_general x24 -> x0, matrix products: 36.4 us -> none  [the longest x8 14.2 us: scores(): jnp.einsum('td,kd->tk', tokens, code_block, preferred_element_type=jnp.fl...]
    convert_element_type x3 -> x0, other arithmetic: 7.98 us -> none  [the longest x1 5.29 us: body(): code_local.astype(jnp.bfloat16)]
    scatter-add x1 -> x0, other arithmetic: 6.36 us -> none  [body(): jax.ops.segment_sum(cotangent.astype(jnp.float32), jnp.where(inside, loca...]
  transfers between devices with their start and end apart: 3 -> 0, of which waited for: 2 -> 0; matrix products, arithmetic and copies ran while one was open for 3% -> 0% of each run, Pallas kernels for 0% -> 0%
where the time goes in v1:
time: 91.9 us; the launch traced here: 91.4 us
  Pallas kernels  82.9 us (90%)
  local copies, waits for them, and re-layouts  6.13 us (7%)
  between operations  2.35 us (3%)
    pallas_call x1, Pallas kernels, final_sums(): pl.pallas_call(functools.partial(sums_kernel, chips, tokens_total, codes_...  43 us
    pallas_call x1, Pallas kernels, row_stats(): pl.pallas_call(functools.partial(stats_kernel, scale, chips), out_shape=j...  19.2 us
    pallas_call x1, Pallas kernels, grads(): pl.pallas_call(functools.partial(grads_kernel, scale, code_rows), grid=(c...  10.5 us
    pallas_call x1, Pallas kernels, totals(): pl.pallas_call(functools.partial(totals_kernel, scale, code_rows), grid=(...  10.2 us
    unnamed x4, local copies, waits for them, and re-layouts  6.13 us

profile of v1, /device:TPU:1, one launch (start us, length us, event | category | flops | bytes accessed | tf_op | source)
XLA Modules:
  0.0 91.4 jit_solution(3825844472831739395)
XLA Ops:
  0.6 10.2 %totals.1 = (f32[4,512]{1,0:T(4,128)}, bf16[512,256]{1,0:T(8,128)(2,1)}) custom-call(bf16[512,256]{1,0:T(8,128)(2,1)} %tok_ref.3, bf16[512,256]{1,0:T(8,128)(2,1)} %cot_ref.3, s32[1,512]{1,0:T(1,128)} %bitcast.4, bf16[4096,256]{1,0:T(8,128)(2,1)} %cb_ref.3), custom_call_target="tpu_custom_call" | custom-call | tf_op jit(solution)/shard_map/totals/pallas_call | solution.py:62
  10.9 19.2 %row_stats.1.st_ref = f32[4,512]{1,0:T(4,128)} custom-call(f32[4,512]{1,0:T(4,128)} %get-tuple-element.16.st_ref), custom_call_target="tpu_custom_call" | custom-call | tf_op jit(solution)/shard_map/row_stats/pallas_call | solution.py:128
  30.1 10.5 %grads.1 = (bf16[4096,256]{1,0:T(8,128)(2,1)}, f32[16,1,256]{2,1,0:T(1,128)}, bf16[512,256]{1,0:T(8,128)(2,1)}) custom-call(bf16[512,256]{1,0:T(8,128)(2,1)} %tok_ref.3, bf16[512,256]{1,0:T(8,128)(2,1)} %cot_ref.3, s32[1,512]{1,0:T(1,128)} %bitcast.5, f32[4,512]{1,0:T(4,128)} %row_stats.1.st_ref, bf16[4096,256]{1,0:T(8,128)(2,1)} %cb_ref.3), custom_call_target="tpu_custom_call" | custom-call | tf_op jit(solution)/shard_map/grads/pallas_call | solution.py:185
  40.6 43.0 %final_sums.1 = (bf16[512,256]{1,0:T(8,128)(2,1)}, bf16[512,256]{1,0:T(8,128)(2,1)}, bf16[256,256]{1,0:T(8,128)(2,1)}, f32[1,256]{1,0:T(1,128)}, f32[1,128]{1,0:T(1,128)}) custom-call(bf16[512,256]{1,0:T(8,128)(2,1)} %get-tuple-element.15.q_ref, bf16[512,256]{1,0:T(8,128)(2,1)} %get-tuple-element.17.tg_ref, bf16[4096,256]{1,0:T(8,128)(2,1)} %get-tuple-element.18.cg_ref, ...), custom_call_target="tpu_custom_call" | custom-call | tf_op jit(solution)/shard_map/final_sums/pallas_call | solution.py:422
  83.6 1.7 %copy.14 = bf16[512,256]{1,0:T(8,128)(2,1)} copy(bf16[512,256]{1,0:T(8,128)(2,1)} %get-tuple-element.30) | data formatting | bytes 524288
  85.2 1.7 %copy.15 = bf16[512,256]{1,0:T(8,128)(2,1)} copy(bf16[512,256]{1,0:T(8,128)(2,1)} %get-tuple-element.31) | data formatting | bytes 524288
  86.9 1.6 %copy.16 = bf16[256,256]{1,0:T(8,128)(2,1)} copy(bf16[256,256]{1,0:T(8,128)(2,1)} %get-tuple-element.32) | data formatting | bytes 262144
  88.5 1.2 %copy.17 = f32[256]{0:T(256)} copy(f32[256]{0:T(256)} %bitcast.6) | data formatting | bytes 2048

commit v2 on v1

v2 whole, which is shorter than its diff:
```python
import functools

import jax
import jax.numpy as jnp
from jax import lax
from jax.experimental import pallas as pl
from jax.experimental.pallas import tpu as pltpu
from jax.sharding import PartitionSpec as P

MESH = pl.DeviceIdType.MESH
F32 = jnp.float32
BF16 = jnp.bfloat16
RING = 4
VMEM_BYTES = 60 * 1024 * 1024


def dot(a, b, dims):
    return lax.dot_general(a, b, (dims, ((), ())), preferred_element_type=F32)


def vmem():
    return pl.BlockSpec(memory_space=pltpu.VMEM)


def fused_kernel(
    scale, code_rows, block, chips, tokens_total, codes_total,
    tok_ref, cot_ref, idx_ref, cb_hbm,
    qo_ref, tgo_ref, cgo_ref, uso_ref, loss_ref,
    cb_ref, w_buf, s_buf, ch_buf, cg_ref, us_ref, tops, run, acc, qt_ref,
    pair_buf, mine_buf, chip_buf, stats,
    t_in, t_half, t_piece, t_sum, t_full,
    x_hop, x_out, x_got, z_part, z_hop, z_out, z_got,
    u_buf, l_own, l_dp, l_core, l_pair, l_chip,
    cb_sem, s_send, s_recv, st_send, st_recv,
    t_send, t_recv, p_send, p_recv, g_send, g_recv, f_send, f_recv,
    x_send, x_recv, z_send, z_recv,
    u_send, u_recv, ld_send, ld_recv, lc_send, lc_recv, lg_send, lg_recv,
):
    dp = lax.axis_index("dp")
    code = lax.axis_index("code")
    core, chip = code % 2, code // 2
    xi, zi = dp // RING, dp % RING
    data = RING * RING
    blocks = code_rows // block
    rows = tok_ref.shape[0]
    half = rows // 2
    piece = half // chips
    span = code_rows // data
    hs = span // 2
    first_code = code * code_rows

    def load(i):
        part = pl.ds(pl.multiple_of(i * block, block), block)
        return pltpu.make_async_copy(cb_hbm.at[part], cb_ref.at[part], cb_sem.at[i])

    for i in range(blocks):
        load(i).start()

    partner = (dp, chip * 2 + 1 - core)
    peers = [(dp, ((chip + j) % chips) * 2 + core) for j in range(1, chips)]
    mates = [((dp + j) % data, code) for j in range(1, data)]
    xn = {d: (((xi + d) % RING) * RING + zi, code) for d in (1, 3)}
    zn = {d: (xi * RING + (zi + d) % RING, code) for d in (1, 3)}

    barrier = pltpu.get_barrier_semaphore()
    for peer in [partner] + peers + mates:
        pl.semaphore_signal(barrier, inc=1, device_id=peer, device_id_type=MESH)

    pending = []

    def send(src, dst, ssem, rsem, peer):
        copy = pltpu.make_async_remote_copy(
            src_ref=src, dst_ref=dst, send_sem=ssem, recv_sem=rsem, device_id=peer, device_id_type=MESH
        )
        copy.start()
        pending.append(copy)
        return copy

    run[0:1, :] = jnp.full((1, rows), -jnp.inf, F32)
    run[1:4, :] = jnp.zeros((3, rows), F32)

    def totals(i, carry):
        load(i).wait()
        part = pl.ds(pl.multiple_of(i * block, block), block)
        codes = cb_ref[part, :]
        logits = dot(codes, tok_ref[...], ((1,), (1,)))
        sensed = dot(codes, cot_ref[...], ((1,), (1,)))
        old = run[0:1, :]
        top = jnp.maximum(old, jnp.max(logits, axis=0, keepdims=True))
        weights = jnp.exp((logits - top) * scale)
        factor = jnp.exp((old - top) * scale)
        w_buf[part, :] = weights
        s_buf[part, :] = sensed
        tops[i] = top
        run[0:1, :] = top
        run[1:2, :] = run[1:2, :] * factor + jnp.sum(weights, axis=0, keepdims=True)
        run[2:3, :] = run[2:3, :] * factor + jnp.sum(weights * sensed, axis=0, keepdims=True)
        run[3:4, :] = run[3:4, :] * factor + jnp.sum(weights * logits, axis=0, keepdims=True)
        return carry

    lax.fori_loop(0, blocks, totals, 0)

    pl.semaphore_wait(barrier, chips + data - 1)
    swap = send(run, pair_buf, s_send, s_recv, partner)

    acc[...] = jnp.zeros_like(acc)

    def picks(i, carry):
        part = pl.ds(pl.multiple_of(i * block, block), block)
        ids = lax.broadcasted_iota(jnp.int32, (block, rows), 0)
        hot = jnp.where(ids == idx_ref[...] - (first_code + i * block), 1.0, 0.0).astype(BF16)
        acc[...] += dot(cb_ref[part, :], hot, ((0,), (0,)))
        ch_buf[part, :] = dot(hot, cot_ref[...], ((1,), (0,)))
        return carry

    lax.fori_loop(0, blocks // 4, picks, 0)

    swap.wait_recv()
    one, two = run[...], pair_buf[...]
    top = jnp.maximum(one[0:1], two[0:1])
    mine_buf[0:1, :] = top
    mine_buf[1:4, :] = one[1:4] * jnp.exp((one[0:1] - top) * scale) + two[1:4] * jnp.exp((two[0:1] - top) * scale)
    st_copies = [
        send(mine_buf, chip_buf.at[chip], st_send.at[j - 1], st_recv.at[j - 1], peers[j - 1])
        for j in range(1, chips)
    ]
    chip_buf[pl.ds(chip, 1), :, :] = mine_buf[...][None]

    lax.fori_loop(blocks // 4, blocks, picks, 0)

    theirs = pl.ds(pl.multiple_of((1 - core) * half, half), half)
    ours = pl.ds(pl.multiple_of(core * half, half), half)

    def rows_of(j):
        return pl.ds(pl.multiple_of(((chip + j) % chips) * piece, piece), piece)

    def t_core(a):
        return send(qt_ref.at[a, theirs], t_in.at[a], t_send.at[a], t_recv.at[a], partner)

    def t_scatter(a, copy):
        copy.wait_recv()
        t_half[a] = (t_in[a].astype(F32) + qt_ref[a, ours, :].astype(F32)).astype(BF16)
        return [
            send(t_half.at[a, rows_of(j)], t_piece.at[a, j], p_send.at[a, j - 1], p_recv.at[a, j - 1], peers[j - 1])
            for j in range(1, chips)
        ]

    def t_gather(a, copies):
        for copy in copies:
            copy.wait_recv()
        total = t_half[a, rows_of(0), :].astype(F32)
        for j in range(1, chips):
            total = total + t_piece[a, j].astype(F32)
        t_sum[a] = total.astype(BF16)
        spot = pl.ds(pl.multiple_of(core * half + chip * piece, piece), piece)
        sent = [
            send(t_sum.at[a], t_full.at[a, spot], g_send.at[a, j - 1], g_recv.at[a, j - 1], peers[j - 1])
            for j in range(1, chips)
        ]
        t_full[a, spot, :] = t_sum[a]
        return sent

    def t_share(a, copies):
        for copy in copies:
            copy.wait_recv()
        return send(t_full.at[a, ours], t_full.at[a, ours], f_send.at[a], f_recv.at[a], partner)

    qt_ref[1] = acc[...].T.astype(BF16)
    q_copy = t_core(1)
    acc[...] = jnp.zeros_like(acc)

    for copy in st_copies:
        copy.wait_recv()
    peaks = [chip_buf[j, 0:1, :] for j in range(chips)]
    peak = functools.reduce(jnp.maximum, peaks)
    total = sum(chip_buf[j, 1:4, :] * jnp.exp((peaks[j] - peak) * scale) for j in range(chips))
    weight = total[0:1]
    stats[0:1, :] = peak
    stats[1:2, :] = 1.0 / weight
    stats[2:3, :] = total[1:2] / weight
    stats[3:4, :] = jnp.log(weight) + (peak - total[2:3] / weight) * scale

    order = [(zi + d) % RING for d in (2, 1, 3, 0)]
    lanes = min(128, rows)

    def units(k, low, high):
        def unit(i, carry):
            owner = ((xi + 6 - i) % RING) * RING + order[k]
            start = owner * span
            part = pl.ds(pl.multiple_of(start, span), span)
            level = jnp.exp((tops[start // block] - stats[0:1, :]) * scale) * stats[1:2, :]
            probs = w_buf[part, :] * level
            grad = (probs * (s_buf[part, :] - stats[2:3, :])).astype(BF16)
            acc[...] += dot(cb_ref[part, :], grad, ((0,), (0,)))
            cg_ref[part, :] = (dot(grad, tok_ref[...], ((1,), (0,))) * scale + ch_buf[part, :]).astype(BF16)
            folded = sum(probs[:, c : c + lanes] for c in range(0, rows, lanes))
            us_ref[owner] = jnp.sum(folded.T, axis=0, keepdims=True)
            return carry

        lax.fori_loop(low, high, unit, 0)

    x_copies = {}
    z_copies = {}

    def part(xd, k, side):
        start = (((xi + xd) % RING) * RING + order[k]) * span + side * hs
        return pl.ds(pl.multiple_of(start, hs), hs)

    def x_first(k):
        x_copies[k, 0] = send(cg_ref.at[part(2, k, 0)], x_hop.at[k, 0], x_send.at[k, 0], x_recv.at[k, 0], xn[1])
        x_copies[k, 1] = send(cg_ref.at[part(2, k, 1)], x_hop.at[k, 1], x_send.at[k, 1], x_recv.at[k, 1], xn[3])

    def x_direct(k):
        x_copies[k, 2] = send(cg_ref.at[part(1, k, 1)], x_got.at[k, 1], x_send.at[k, 2], x_recv.at[k, 2], xn[1])
        x_copies[k, 3] = send(cg_ref.at[part(3, k, 0)], x_got.at[k, 0], x_send.at[k, 3], x_recv.at[k, 3], xn[3])

    def x_second(k):
        x_copies[k, 0].wait_recv()
        x_out[k, 0] = (x_hop[k, 0].astype(F32) + cg_ref[part(1, k, 0), :].astype(F32)).astype(BF16)
        x_copies[k, 4] = send(x_out.at[k, 0], x_got.at[k, 3], x_send.at[k, 4], x_recv.at[k, 4], xn[1])
        x_copies[k, 1].wait_recv()
        x_out[k, 1] = (x_hop[k, 1].astype(F32) + cg_ref[part(3, k, 1), :].astype(F32)).astype(BF16)
        x_copies[k, 5] = send(x_out.at[k, 1], x_got.at[k, 2], x_send.at[k, 5], x_recv.at[k, 5], xn[3])

    def x_third(k):
        for i in (2, 3, 4, 5):
            x_copies[k, i].wait_recv()
        low = cg_ref[part(0, k, 0), :].astype(F32) + x_got[k, 0].astype(F32) + x_got[k, 3].astype(F32)
        high = cg_ref[part(0, k, 1), :].astype(F32) + x_got[k, 1].astype(F32) + x_got[k, 2].astype(F32)
        return low, high

    def z_store(k):
        low, high = x_third(k)
        z_part[k, 0] = low.astype(BF16)
        z_part[k, 1] = high.astype(BF16)

    def z_first():
        z_store(0)
        z_copies[0] = send(z_part.at[0, 0], z_hop.at[0], z_send.at[0], z_recv.at[0], zn[1])
        z_copies[1] = send(z_part.at[0, 1], z_hop.at[1], z_send.at[1], z_recv.at[1], zn[3])

    def z_second_up():
        z_store(1)
        z_copies[2] = send(z_part.at[1, 1], z_got.at[1], z_send.at[2], z_recv.at[2], zn[1])
        z_copies[0].wait_recv()
        z_out[0] = (z_hop[0].astype(F32) + z_part[1, 0].astype(F32)).astype(BF16)
        z_copies[4] = send(z_out.at[0], z_got.at[3], z_send.at[4], z_recv.at[4], zn[1])

    def z_second_down():
        z_store(2)
        z_copies[3] = send(z_part.at[2, 0], z_got.at[0], z_send.at[3], z_recv.at[3], zn[3])
        z_copies[1].wait_recv()
        z_out[1] = (z_hop[1].astype(F32) + z_part[2, 1].astype(F32)).astype(BF16)
        z_copies[5] = send(z_out.at[1], z_got.at[2], z_send.at[5], z_recv.at[5], zn[3])

    def z_third():
        low, high = x_third(3)
        for i in (2, 3, 4, 5):
            z_copies[i].wait_recv()
        cgo_ref[0:hs, :] = (low + z_got[0].astype(F32) + z_got[3].astype(F32)).astype(BF16)
        cgo_ref[hs:, :] = (high + z_got[1].astype(F32) + z_got[2].astype(F32)).astype(BF16)

    units(0, 0, 1)
    x_first(0)
    q_copies = t_scatter(1, q_copy)
    units(0, 1, 4)
    x_direct(0)
    units(1, 0, 4)
    x_first(1)
    x_second(0)
    x_direct(1)
    q_copies = t_gather(1, q_copies)
    units(2, 0, 4)
    x_first(2)
    x_second(1)
    x_direct(2)
    q_copy = t_share(1, q_copies)
    units(3, 0, 4)

    qt_ref[0] = (acc[...] * scale).T.astype(BF16)
    g_copy = t_core(0)
    u_copies = [
        send(us_ref.at[(dp + j) % data], u_buf.at[dp], u_send.at[j - 1], u_recv.at[j - 1], mates[j - 1])
        for j in range(1, data)
    ]
    u_buf[pl.ds(dp, 1), :, :] = us_ref[pl.ds(dp, 1), :, :]
    x_first(3)
    x_second(2)
    x_direct(3)
    g_copies = t_scatter(0, g_copy)
    z_first()

    for copy in u_copies:
        copy.wait_recv()
    usage = sum(u_buf[j] for j in range(data))
    uso_ref[...] = usage * (codes_total / tokens_total)
    shares = usage / tokens_total
    terms = jnp.where(shares > 0, shares * jnp.log(jnp.where(shares > 0, shares, 1.0)), 0.0)
    local = jnp.sum(stats[3:4, :]) / (tokens_total * chips * 2) + jnp.sum(terms)
    l_own[...] = jnp.full(l_own.shape, local, F32)
    l_dp[pl.ds(dp, 1), :, :] = l_own[...][None]
    ld_copies = [
        send(l_own, l_dp.at[dp], ld_send.at[j - 1], ld_recv.at[j - 1], mates[j - 1]) for j in range(1, data)
    ]

    x_second(3)
    z_second_up()
    g_copies = t_gather(0, g_copies)

    for copy in ld_copies:
        copy.wait_recv()
    l_core[...] = sum(l_dp[j] for j in range(data))
    lc_copy = send(l_core, l_pair, lc_send, lc_recv, partner)

    z_second_down()
    g_copy = t_share(0, g_copies)

    lc_copy.wait_recv()
    l_chip[pl.ds(chip, 1), :, :] = (l_core[...] + l_pair[...])[None]
    lg_copies = [
        send(l_chip.at[chip], l_chip.at[chip], lg_send.at[j - 1], lg_recv.at[j - 1], peers[j - 1])
        for j in range(1, chips)
    ]

    q_copy.wait_recv()
    qo_ref[...] = t_full[1]
    z_third()
    g_copy.wait_recv()
    tgo_ref[...] = t_full[0]
    for copy in lg_copies:
        copy.wait_recv()
    loss_ref[...] = sum(l_chip[j] for j in range(chips))

    for copy in pending:
        copy.wait_send()


def fused(tokens, cotangent, index, codebook, scale, block, chips, tokens_total, codes_total):
    rows, width = tokens.shape
    code_rows = codebook.shape[0]
    data = RING * RING
    span = code_rows // data
    hs = span // 2
    half = rows // 2
    piece = half // chips
    blocks = code_rows // block
    dma = pltpu.SemaphoreType.DMA
    return pl.pallas_call(
        functools.partial(fused_kernel, scale, code_rows, block, chips, tokens_total, codes_total),
        out_shape=(
            jax.ShapeDtypeStruct((rows, width), BF16),
            jax.ShapeDtypeStruct((rows, width), BF16),
            jax.ShapeDtypeStruct((span, width), BF16),
            jax.ShapeDtypeStruct((1, span), F32),
            jax.ShapeDtypeStruct((1, 128), F32),
        ),
        in_specs=[vmem()] * 3 + [pl.BlockSpec(memory_space=pl.ANY)],
        out_specs=(vmem(),) * 5,
        scratch_shapes=[
            pltpu.VMEM((code_rows, width), BF16),
            pltpu.VMEM((code_rows, rows), F32),
            pltpu.VMEM((code_rows, rows), F32),
            pltpu.VMEM((code_rows, width), F32),
            pltpu.VMEM((code_rows, width), BF16),
            pltpu.VMEM((data, 1, span), F32),
            pltpu.VMEM((blocks, 1, rows), F32),
            pltpu.VMEM((4, rows), F32),
            pltpu.VMEM((width, rows), F32),
            pltpu.VMEM((2, rows, width), BF16),
            pltpu.VMEM((4, rows), F32),
            pltpu.VMEM((4, rows), F32),
            pltpu.VMEM((chips, 4, rows), F32),
            pltpu.VMEM((4, rows), F32),
            pltpu.VMEM((2, half, width), BF16),
            pltpu.VMEM((2, half, width), BF16),
            pltpu.VMEM((2, chips, piece, width), BF16),
            pltpu.VMEM((2, piece, width), BF16),
            pltpu.VMEM((2, rows, width), BF16),
            pltpu.VMEM((RING, 2, hs, width), BF16),
            pltpu.VMEM((RING, 2, hs, width), BF16),
            pltpu.VMEM((RING, 4, hs, width), BF16),
            pltpu.VMEM((RING - 1, 2, hs, width), BF16),
            pltpu.VMEM((2, hs, width), BF16),
            pltpu.VMEM((2, hs, width), BF16),
            pltpu.VMEM((4, hs, width), BF16),
            pltpu.VMEM((data, 1, span), F32),
            pltpu.VMEM((1, 128), F32),
            pltpu.VMEM((data, 1, 128), F32),
            pltpu.VMEM((1, 128), F32),
            pltpu.VMEM((1, 128), F32),
            pltpu.VMEM((chips, 1, 128), F32),
            dma((blocks,)),
            dma, dma,
            dma((chips - 1,)), dma((chips - 1,)),
            dma((2,)), dma((2,)),
            dma((2, chips - 1)), dma((2, chips - 1)),
            dma((2, chips - 1)), dma((2, chips - 1)),
            dma((2,)), dma((2,)),
            dma((RING, 6)), dma((RING, 6)),
            dma((6,)), dma((6,)),
            dma((data - 1,)), dma((data - 1,)),
            dma((data - 1,)), dma((data - 1,)),
            dma, dma,
            dma((chips - 1,)), dma((chips - 1,)),
        ],
        compiler_params=pltpu.CompilerParams(
            collective_id=0, has_side_effects=True, vmem_limit_bytes=VMEM_BYTES
        ),
        name="fused",
    )(tokens, cotangent, index, codebook)


def finish_kernel(*refs):
    count = len(refs) // 2
    for source, target in zip(refs[:count], refs[count:]):
        target[...] = source[...]


def finish(*arrays):
    return pl.pallas_call(
        finish_kernel,
        out_shape=tuple(jax.ShapeDtypeStruct(a.shape, a.dtype) for a in arrays),
        in_specs=[vmem()] * len(arrays),
        out_specs=(vmem(),) * len(arrays),
        name="finish",
    )(*arrays)


def body(block, tokens, codebook, cotangent, index):
    token_rows, features = tokens.shape
    code_rows = codebook.shape[0]
    scale = float(features) ** (-0.5)
    code_devices = lax.axis_size("code")
    data_devices = lax.axis_size("dp")
    results = fused(
        tokens, cotangent, index.reshape(1, token_rows), codebook, scale, block, code_devices // 2,
        token_rows * data_devices, code_rows * code_devices,
    )
    quantized, token_grad, code_sum, code_usage, loss = finish(*results)
    return (quantized, token_grad, code_sum, code_usage.reshape(-1), loss[0, 0])


def solution(mesh, block=512):
    placed = (P("dp", None), P("code", None), P("dp", None), P("dp"))
    return jax.shard_map(
        functools.partial(body, block),
        mesh=mesh,
        in_specs=placed,
        out_specs=(P("dp", None), P("dp", None), P(("code", "dp"), None), P(("code", "dp")), P()),
        check_vma=False,
    )
```

time: 91.9 us -> 69.1 us (0.75)
  Pallas kernels: 82.9 us -> 67.6 us
  local copies, waits for them, and re-layouts: 6.13 us -> 0 us
  between operations: 2.35 us -> 0.64 us
    pallas_call x4 -> x2, Pallas kernels: 82.9 us -> 67.6 us  [the longest x1 65.6 us: fused(): pl.pallas_call(functools.partial(fused_kernel, scale, code_rows, block, c...]
    unnamed x4 -> x0, local copies, waits for them, and re-layouts: 6.13 us -> none
where the time goes in v2:
time: 69.1 us; the launch traced here: 68.2 us
  Pallas kernels  67.6 us (98%)
    pallas_call x1, Pallas kernels, fused(): pl.pallas_call(functools.partial(fused_kernel, scale, code_rows, block, c...  65.6 us
    pallas_call x1, Pallas kernels, finish(): pl.pallas_call(finish_kernel, out_shape=tuple((jax.ShapeDtypeStruct(a.sha...  1.92 us

profile of v2, /device:TPU:1, one launch (start us, length us, event | category | flops | bytes accessed | tf_op | source)
XLA Modules:
  0.0 68.2 jit_solution(6989926428725356317)
XLA Ops:
  0.6 65.6 %fused.1 = (bf16[512,256]{1,0:T(8,128)(2,1)}, bf16[512,256]{1,0:T(8,128)(2,1)}, bf16[256,256]{1,0:T(8,128)(2,1)}, f32[1,256]{1,0:T(1,128)}, f32[1,128]{1,0:T(1,128)}) custom-call(bf16[512,256]{1,0:T(8,128)(2,1)} %tok_ref.1, bf16[512,256]{1,0:T(8,128)(2,1)} %cot_ref.1, s32[1,512]{1,0:T(1,128)} %bitcast.4, bf16[4096,256]{1,0:T(8,128)(2,1)} %cb_hbm.1), custom_call_target="tpu_custom_call" | custom-call | tf_op jit(solution)/shard_map/fused/pallas_call | solution.py:348
  66.3 1.9 %finish.1 = (bf16[512,256]{1,0:T(8,128)(2,1)}, bf16[512,256]{1,0:T(8,128)(2,1)}, bf16[256,256]{1,0:T(8,128)(2,1)}, f32[1,256]{1,0:T(1,128)}, f32[1,128]{1,0:T(1,128)}) custom-call(bf16[512,256]{1,0:T(8,128)(2,1)} %get-tuple-element.15.refs_0_, bf16[512,256]{1,0:T(8,128)(2,1)} %get-tuple-element.16.refs_1_, bf16[256,256]{1,0:T(8,128)(2,1)} %get-tuple-element.17.refs_2_, ...), custom_call_target="tpu_custom_call" | custom-call | tf_op jit(solution)/shard_map/finish/pallas_call | solution.py:420

commit v3 on v2

--- a/solution.py
+++ b/solution.py
@@ -30,11 +30,11 @@
     pair_buf, mine_buf, chip_buf, stats,
     t_in, t_half, t_piece, t_sum, t_full,
     x_hop, x_out, x_got, z_part, z_hop, z_out, z_got,
-    u_buf, l_own, l_dp, l_core, l_pair, l_chip,
+    u_buf, l_own, l_all, l_dp, l_core, l_pair, l_chip,
     cb_sem, s_send, s_recv, st_send, st_recv,
     t_send, t_recv, p_send, p_recv, g_send, g_recv, f_send, f_recv,
     x_send, x_recv, z_send, z_recv,
-    u_send, u_recv, ld_send, ld_recv, lc_send, lc_recv, lg_send, lg_recv,
+    u_sems, ld_send, ld_recv, lc_send, lc_recv, lg_send, lg_recv,
 ):
     dp = lax.axis_index("dp")
     code = lax.axis_index("code")
@@ -197,7 +197,7 @@
             us_ref[owner] = jnp.sum(folded.T, axis=0, keepdims=True)
             return carry
 
-        lax.fori_loop(low, high, unit, 0)
+        lax.fori_loop(low, high, unit, 0, unroll=True)
 
     x_copies = {}
     z_copies = {}
@@ -260,35 +260,44 @@
         cgo_ref[0:hs, :] = (low + z_got[0].astype(F32) + z_got[3].astype(F32)).astype(BF16)
         cgo_ref[hs:, :] = (high + z_got[1].astype(F32) + z_got[2].astype(F32)).astype(BF16)
 
+    u_copies = []
+
+    def u_send(k):
+        for xd in range(RING if k < RING - 1 else 1, 2 * RING if k < RING - 1 else RING):
+            owner = ((xi + xd) % RING) * RING + order[k]
+            slot = k * RING + xd % RING
+            u_copies.append(
+                send(us_ref.at[owner], u_buf.at[dp], u_sems.at[0, slot], u_sems.at[1, slot], (owner, code))
+            )
+
     units(0, 0, 1)
     x_first(0)
     q_copies = t_scatter(1, q_copy)
     units(0, 1, 4)
+    u_send(0)
     x_direct(0)
     units(1, 0, 4)
+    u_send(1)
     x_first(1)
     x_second(0)
     x_direct(1)
+    units(2, 0, 4)
+    u_send(2)
+    x_first(2)
     q_copies = t_gather(1, q_copies)
-    units(2, 0, 4)
-    x_first(2)
+    units(3, 0, 4)
+    u_send(3)
+    qt_ref[0] = (acc[...] * scale).T.astype(BF16)
+    g_copy = t_core(0)
+    u_buf[pl.ds(dp, 1), :, :] = us_ref[pl.ds(dp, 1), :, :]
     x_second(1)
     x_direct(2)
+    x_first(3)
+    g_copies = t_scatter(0, g_copy)
     q_copy = t_share(1, q_copies)
-    units(3, 0, 4)
-
-    qt_ref[0] = (acc[...] * scale).T.astype(BF16)
-    g_copy = t_core(0)
-    u_copies = [
-        send(us_ref.at[(dp + j) % data], u_buf.at[dp], u_send.at[j - 1], u_recv.at[j - 1], mates[j - 1])
-        for j in range(1, data)
-    ]
-    u_buf[pl.ds(dp, 1), :, :] = us_ref[pl.ds(dp, 1), :, :]
-    x_first(3)
+    z_first()
     x_second(2)
     x_direct(3)
-    g_copies = t_scatter(0, g_copy)
-    z_first()
 
     for copy in u_copies:
         copy.wait_recv()
@@ -297,39 +306,34 @@
     shares = usage / tokens_total
     terms = jnp.where(shares > 0, shares * jnp.log(jnp.where(shares > 0, shares, 1.0)), 0.0)
     local = jnp.sum(stats[3:4, :]) / (tokens_total * chips * 2) + jnp.sum(terms)
-    l_own[...] = jnp.full(l_own.shape, local, F32)
-    l_dp[pl.ds(dp, 1), :, :] = l_own[...][None]
+    l_core[...] = jnp.full(l_core.shape, local, F32)
+    lc_copy = send(l_core, l_pair, lc_send, lc_recv, partner)
+    z_second_up()
+    lc_copy.wait_recv()
+    l_own[...] = l_core[...] + l_pair[...]
+    l_chip[pl.ds(chip, 1), :, :] = l_own[...][None]
+    lg_copies = [
+        send(l_own, l_chip.at[chip], lg_send.at[j - 1], lg_recv.at[j - 1], peers[j - 1]) for j in range(1, chips)
+    ]
+    x_second(3)
+    g_copies = t_gather(0, g_copies)
+    z_second_down()
+    for copy in lg_copies:
+        copy.wait_recv()
+    l_all[...] = sum(l_chip[j] for j in range(chips))
+    l_dp[pl.ds(dp, 1), :, :] = l_all[...][None]
     ld_copies = [
-        send(l_own, l_dp.at[dp], ld_send.at[j - 1], ld_recv.at[j - 1], mates[j - 1]) for j in range(1, data)
+        send(l_all, l_dp.at[dp], ld_send.at[j - 1], ld_recv.at[j - 1], mates[j - 1]) for j in range(1, data)
     ]
-
-    x_second(3)
-    z_second_up()
-    g_copies = t_gather(0, g_copies)
-
-    for copy in ld_copies:
-        copy.wait_recv()
-    l_core[...] = sum(l_dp[j] for j in range(data))
-    lc_copy = send(l_core, l_pair, lc_send, lc_recv, partner)
-
-    z_second_down()
-    g_copy = t_share(0, g_copies)
-
-    lc_copy.wait_recv()
-    l_chip[pl.ds(chip, 1), :, :] = (l_core[...] + l_pair[...])[None]
-    lg_copies = [
-        send(l_chip.at[chip], l_chip.at[chip], lg_send.at[j - 1], lg_recv.at[j - 1], peers[j - 1])
-        for j in range(1, chips)
-    ]
-
     q_copy.wait_recv()
     qo_ref[...] = t_full[1]
     z_third()
+    g_copy = t_share(0, g_copies)
+    for copy in ld_copies:
+        copy.wait_recv()
+    loss_ref[...] = sum(l_dp[j] for j in range(data))
     g_copy.wait_recv()
     tgo_ref[...] = t_full[0]
-    for copy in lg_copies:
-        copy.wait_recv()
-    loss_ref[...] = sum(l_chip[j] for j in range(chips))
 
     for copy in pending:
         copy.wait_send()
@@ -385,6 +389,7 @@
             pltpu.VMEM((4, hs, width), BF16),
             pltpu.VMEM((data, 1, span), F32),
             pltpu.VMEM((1, 128), F32),
+            pltpu.VMEM((1, 128), F32),
             pltpu.VMEM((data, 1, 128), F32),
             pltpu.VMEM((1, 128), F32),
             pltpu.VMEM((1, 128), F32),
@@ -398,7 +403,7 @@
             dma((2,)), dma((2,)),
             dma((RING, 6)), dma((RING, 6)),
             dma((6,)), dma((6,)),
-            dma((data - 1,)), dma((data - 1,)),
+            dma((2, data)),
             dma((data - 1,)), dma((data - 1,)),
             dma, dma,
             dma((chips - 1,)), dma((chips - 1,)),

time: 69.1 us -> 61.6 us (0.89)
  Pallas kernels: 67.6 us -> 60.6 us
    pallas_call x1, Pallas kernels: 65.6 us -> 58.6 us  [fused(): pl.pallas_call(functools.partial(fused_kernel, scale, code_rows, block, c...]
where the time goes in v3:
time: 61.6 us; the launch traced here: 61.2 us
  Pallas kernels  60.6 us (98%)
  between operations  0.64 us (1%)
    pallas_call x1, Pallas kernels, fused(): pl.pallas_call(functools.partial(fused_kernel, scale, code_rows, block, c...  58.6 us
    pallas_call x1, Pallas kernels, finish(): pl.pallas_call(finish_kernel, out_shape=tuple((jax.ShapeDtypeStruct(a.sha...  1.92 us

profile of v3, /device:TPU:1, one launch (start us, length us, event | category | flops | bytes accessed | tf_op | source)
XLA Modules:
  0.0 61.2 jit_solution(3675774677631561416)
XLA Ops:
  0.6 58.6 %fused.1 = (bf16[512,256]{1,0:T(8,128)(2,1)}, bf16[512,256]{1,0:T(8,128)(2,1)}, bf16[256,256]{1,0:T(8,128)(2,1)}, f32[1,256]{1,0:T(1,128)}, f32[1,128]{1,0:T(1,128)}) custom-call(bf16[512,256]{1,0:T(8,128)(2,1)} %tok_ref.1, bf16[512,256]{1,0:T(8,128)(2,1)} %cot_ref.1, s32[1,512]{1,0:T(1,128)} %bitcast.4, bf16[4096,256]{1,0:T(8,128)(2,1)} %cb_hbm.1), custom_call_target="tpu_custom_call" | custom-call | tf_op jit(solution)/shard_map/fused/pallas_call | solution.py:352
  59.3 1.9 %finish.1 = (bf16[512,256]{1,0:T(8,128)(2,1)}, bf16[512,256]{1,0:T(8,128)(2,1)}, bf16[256,256]{1,0:T(8,128)(2,1)}, f32[1,256]{1,0:T(1,128)}, f32[1,128]{1,0:T(1,128)}) custom-call(bf16[512,256]{1,0:T(8,128)(2,1)} %get-tuple-element.15.refs_0_, bf16[512,256]{1,0:T(8,128)(2,1)} %get-tuple-element.16.refs_1_, bf16[256,256]{1,0:T(8,128)(2,1)} %get-tuple-element.17.refs_2_, ...), custom_call_target="tpu_custom_call" | custom-call | tf_op jit(solution)/shard_map/finish/pallas_call | solution.py:425

commit v4 on v3

--- a/solution.py
+++ b/solution.py
@@ -193,11 +193,17 @@
             grad = (probs * (s_buf[part, :] - stats[2:3, :])).astype(BF16)
             acc[...] += dot(cb_ref[part, :], grad, ((0,), (0,)))
             cg_ref[part, :] = (dot(grad, tok_ref[...], ((1,), (0,))) * scale + ch_buf[part, :]).astype(BF16)
-            folded = sum(probs[:, c : c + lanes] for c in range(0, rows, lanes))
-            us_ref[owner] = jnp.sum(folded.T, axis=0, keepdims=True)
             return carry
 
         lax.fori_loop(low, high, unit, 0, unroll=True)
+
+    def usage_of(owner, carry):
+        start = owner * span
+        level = jnp.exp((tops[start // block] - stats[0:1, :]) * scale) * stats[1:2, :]
+        probs = w_buf[pl.ds(pl.multiple_of(start, span), span), :] * level
+        folded = sum(probs[:, c : c + lanes] for c in range(0, rows, lanes))
+        us_ref[owner] = jnp.sum(folded.T, axis=0, keepdims=True)
+        return carry
 
     x_copies = {}
     z_copies = {}
@@ -260,44 +266,29 @@
         cgo_ref[0:hs, :] = (low + z_got[0].astype(F32) + z_got[3].astype(F32)).astype(BF16)
         cgo_ref[hs:, :] = (high + z_got[1].astype(F32) + z_got[2].astype(F32)).astype(BF16)
 
-    u_copies = []
-
-    def u_send(k):
-        for xd in range(RING if k < RING - 1 else 1, 2 * RING if k < RING - 1 else RING):
-            owner = ((xi + xd) % RING) * RING + order[k]
-            slot = k * RING + xd % RING
-            u_copies.append(
-                send(us_ref.at[owner], u_buf.at[dp], u_sems.at[0, slot], u_sems.at[1, slot], (owner, code))
-            )
-
     units(0, 0, 1)
     x_first(0)
+
+    lax.fori_loop(0, data, usage_of, 0, unroll=4)
+    u_copies = [
+        send(us_ref.at[(dp + j) % data], u_buf.at[dp], u_sems.at[0, j], u_sems.at[1, j], mates[j - 1])
+        for j in range(1, data)
+    ]
+    u_buf[pl.ds(dp, 1), :, :] = us_ref[pl.ds(dp, 1), :, :]
+
     q_copies = t_scatter(1, q_copy)
     units(0, 1, 4)
-    u_send(0)
     x_direct(0)
     units(1, 0, 4)
-    u_send(1)
     x_first(1)
     x_second(0)
     x_direct(1)
     units(2, 0, 4)
-    u_send(2)
     x_first(2)
     q_copies = t_gather(1, q_copies)
     units(3, 0, 4)
-    u_send(3)
     qt_ref[0] = (acc[...] * scale).T.astype(BF16)
     g_copy = t_core(0)
-    u_buf[pl.ds(dp, 1), :, :] = us_ref[pl.ds(dp, 1), :, :]
-    x_second(1)
-    x_direct(2)
-    x_first(3)
-    g_copies = t_scatter(0, g_copy)
-    q_copy = t_share(1, q_copies)
-    z_first()
-    x_second(2)
-    x_direct(3)
 
     for copy in u_copies:
         copy.wait_recv()
@@ -308,16 +299,21 @@
     local = jnp.sum(stats[3:4, :]) / (tokens_total * chips * 2) + jnp.sum(terms)
     l_core[...] = jnp.full(l_core.shape, local, F32)
     lc_copy = send(l_core, l_pair, lc_send, lc_recv, partner)
-    z_second_up()
+
+    x_second(1)
+    x_direct(2)
+    x_first(3)
+    g_copies = t_scatter(0, g_copy)
     lc_copy.wait_recv()
     l_own[...] = l_core[...] + l_pair[...]
     l_chip[pl.ds(chip, 1), :, :] = l_own[...][None]
     lg_copies = [
         send(l_own, l_chip.at[chip], lg_send.at[j - 1], lg_recv.at[j - 1], peers[j - 1]) for j in range(1, chips)
     ]
-    x_second(3)
-    g_copies = t_gather(0, g_copies)
-    z_second_down()
+    z_first()
+    x_second(2)
+    x_direct(3)
+    q_copy = t_share(1, q_copies)
     for copy in lg_copies:
         copy.wait_recv()
     l_all[...] = sum(l_chip[j] for j in range(chips))
@@ -325,10 +321,14 @@
     ld_copies = [
         send(l_all, l_dp.at[dp], ld_send.at[j - 1], ld_recv.at[j - 1], mates[j - 1]) for j in range(1, data)
     ]
+    z_second_up()
+    x_second(3)
+    g_copies = t_gather(0, g_copies)
+    z_second_down()
     q_copy.wait_recv()
     qo_ref[...] = t_full[1]
+    g_copy = t_share(0, g_copies)
     z_third()
-    g_copy = t_share(0, g_copies)
     for copy in ld_copies:
         copy.wait_recv()
     loss_ref[...] = sum(l_dp[j] for j in range(data))

time: 61.6 us -> 61.3 us (level)
  no operation moved by 1% of the time
where the time goes in v4:
time: 61.3 us; the launch traced here: 61.1 us
  Pallas kernels  60.5 us (99%)
  between operations  0.64 us (1%)
    pallas_call x1, Pallas kernels, fused(): pl.pallas_call(functools.partial(fused_kernel, scale, code_rows, block, c...  58.6 us
    pallas_call x1, Pallas kernels, finish(): pl.pallas_call(finish_kernel, out_shape=tuple((jax.ShapeDtypeStruct(a.sha...  1.92 us

profile of v4, /device:TPU:1, one launch (start us, length us, event | category | flops | bytes accessed | tf_op | source)
XLA Modules:
  0.0 61.1 jit_solution(12623316700568820486)
XLA Ops:
  0.6 58.6 %fused.1 = (bf16[512,256]{1,0:T(8,128)(2,1)}, bf16[512,256]{1,0:T(8,128)(2,1)}, bf16[256,256]{1,0:T(8,128)(2,1)}, f32[1,256]{1,0:T(1,128)}, f32[1,128]{1,0:T(1,128)}) custom-call(bf16[512,256]{1,0:T(8,128)(2,1)} %tok_ref.1, bf16[512,256]{1,0:T(8,128)(2,1)} %cot_ref.1, s32[1,512]{1,0:T(1,128)} %bitcast.4, bf16[4096,256]{1,0:T(8,128)(2,1)} %cb_hbm.1), custom_call_target="tpu_custom_call" | custom-call | tf_op jit(solution)/shard_map/fused/pallas_call | solution.py:352
  59.2 1.9 %finish.1 = (bf16[512,256]{1,0:T(8,128)(2,1)}, bf16[512,256]{1,0:T(8,128)(2,1)}, bf16[256,256]{1,0:T(8,128)(2,1)}, f32[1,256]{1,0:T(1,128)}, f32[1,128]{1,0:T(1,128)}) custom-call(bf16[512,256]{1,0:T(8,128)(2,1)} %get-tuple-element.15.refs_0_, bf16[512,256]{1,0:T(8,128)(2,1)} %get-tuple-element.16.refs_1_, bf16[256,256]{1,0:T(8,128)(2,1)} %get-tuple-element.17.refs_2_, ...), custom_call_target="tpu_custom_call" | custom-call | tf_op jit(solution)/shard_map/finish/pallas_call | solution.py:425

commit v5 on v4

--- a/solution.py
+++ b/solution.py
@@ -26,7 +26,7 @@
     scale, code_rows, block, chips, tokens_total, codes_total,
     tok_ref, cot_ref, idx_ref, cb_hbm,
     qo_ref, tgo_ref, cgo_ref, uso_ref, loss_ref,
-    cb_ref, w_buf, s_buf, ch_buf, cg_ref, us_ref, tops, run, acc, qt_ref,
+    cb_ref, l_buf, w_buf, s_buf, ch_buf, cg_ref, us_ref, tops, run, acc, qt_ref,
     pair_buf, mine_buf, chip_buf, stats,
     t_in, t_half, t_piece, t_sum, t_full,
     x_hop, x_out, x_got, z_part, z_hop, z_out, z_got,
@@ -79,26 +79,37 @@
     run[0:1, :] = jnp.full((1, rows), -jnp.inf, F32)
     run[1:4, :] = jnp.zeros((3, rows), F32)
 
-    def totals(i, carry):
+    strip = min(64, block)
+
+    def products(i):
         load(i).wait()
-        part = pl.ds(pl.multiple_of(i * block, block), block)
+        part = slice(i * block, (i + 1) * block)
         codes = cb_ref[part, :]
-        logits = dot(codes, tok_ref[...], ((1,), (1,)))
-        sensed = dot(codes, cot_ref[...], ((1,), (1,)))
+        l_buf[i % 2] = dot(codes, tok_ref[...], ((1,), (1,)))
+        s_buf[part, :] = dot(codes, cot_ref[...], ((1,), (1,)))
+
+    def totals(i):
         old = run[0:1, :]
-        top = jnp.maximum(old, jnp.max(logits, axis=0, keepdims=True))
-        weights = jnp.exp((logits - top) * scale)
+        top = jnp.maximum(old, jnp.max(l_buf[i % 2], axis=0, keepdims=True))
         factor = jnp.exp((old - top) * scale)
-        w_buf[part, :] = weights
-        s_buf[part, :] = sensed
+        sums = [jnp.zeros((8, rows), F32)] * 3
+        for low in range(0, block, strip):
+            part = slice(i * block + low, i * block + low + strip)
+            logits = l_buf[i % 2, low : low + strip, :]
+            weights = jnp.exp2((logits - top) * (scale * 1.4426950408889634))
+            w_buf[part, :] = weights
+            for n, term in enumerate((weights, weights * s_buf[part, :], weights * logits)):
+                sums[n] = sums[n] + jnp.sum(term.reshape(strip // 8, 8, rows), axis=0)
         tops[i] = top
         run[0:1, :] = top
-        run[1:2, :] = run[1:2, :] * factor + jnp.sum(weights, axis=0, keepdims=True)
-        run[2:3, :] = run[2:3, :] * factor + jnp.sum(weights * sensed, axis=0, keepdims=True)
-        run[3:4, :] = run[3:4, :] * factor + jnp.sum(weights * logits, axis=0, keepdims=True)
-        return carry
-
-    lax.fori_loop(0, blocks, totals, 0)
+        for n in range(3):
+            run[n + 1 : n + 2, :] = run[n + 1 : n + 2, :] * factor + jnp.sum(sums[n], axis=0, keepdims=True)
+
+    products(0)
+    for i in range(blocks):
+        if i + 1 < blocks:
+            products(i + 1)
+        totals(i)
 
     pl.semaphore_wait(barrier, chips + data - 1)
     swap = send(run, pair_buf, s_send, s_recv, partner)
@@ -362,6 +373,7 @@
         out_specs=(vmem(),) * 5,
         scratch_shapes=[
             pltpu.VMEM((code_rows, width), BF16),
+            pltpu.VMEM((2, block, rows), F32),
             pltpu.VMEM((code_rows, rows), F32),
             pltpu.VMEM((code_rows, rows), F32),
             pltpu.VMEM((code_rows, width), F32),

time: 61.3 us -> 59.6 us (0.972)
  Pallas kernels: 60.5 us -> 58.8 us
    pallas_call x1, Pallas kernels: 58.6 us -> 56.9 us  [fused(): pl.pallas_call(functools.partial(fused_kernel, scale, code_rows, block, c...]
where the time goes in v5:
time: 59.6 us; the launch traced here: 59.5 us
  Pallas kernels  58.8 us (99%)
  between operations  0.64 us (1%)
    pallas_call x1, Pallas kernels, fused(): pl.pallas_call(functools.partial(fused_kernel, scale, code_rows, block, c...  56.9 us
    pallas_call x1, Pallas kernels, finish(): pl.pallas_call(finish_kernel, out_shape=tuple((jax.ShapeDtypeStruct(a.sha...  1.92 us

profile of v5, /device:TPU:1, one launch (start us, length us, event | category | flops | bytes accessed | tf_op | source)
XLA Modules:
  0.0 59.5 jit_solution(16653570496748644174)
XLA Ops:
  0.6 56.9 %fused.1 = (bf16[512,256]{1,0:T(8,128)(2,1)}, bf16[512,256]{1,0:T(8,128)(2,1)}, bf16[256,256]{1,0:T(8,128)(2,1)}, f32[1,256]{1,0:T(1,128)}, f32[1,128]{1,0:T(1,128)}) custom-call(bf16[512,256]{1,0:T(8,128)(2,1)} %tok_ref.1, bf16[512,256]{1,0:T(8,128)(2,1)} %cot_ref.1, s32[1,512]{1,0:T(1,128)} %bitcast.4, bf16[4096,256]{1,0:T(8,128)(2,1)} %cb_hbm.1), custom_call_target="tpu_custom_call" | custom-call | tf_op jit(solution)/shard_map/fused/pallas_call | solution.py:363
  57.5 1.9 %finish.1 = (bf16[512,256]{1,0:T(8,128)(2,1)}, bf16[512,256]{1,0:T(8,128)(2,1)}, bf16[256,256]{1,0:T(8,128)(2,1)}, f32[1,256]{1,0:T(1,128)}, f32[1,128]{1,0:T(1,128)}) custom-call(bf16[512,256]{1,0:T(8,128)(2,1)} %get-tuple-element.15.refs_0_, bf16[512,256]{1,0:T(8,128)(2,1)} %get-tuple-element.16.refs_1_, bf16[256,256]{1,0:T(8,128)(2,1)} %get-tuple-element.17.refs_2_, ...), custom_call_target="tpu_custom_call" | custom-call | tf_op jit(solution)/shard_map/finish/pallas_call | solution.py:437
